TPU v7x, 32 devices: a whole 2x2x4 slice. The times are simulated.
32 devices in a mesh: frame: 8 (over z, y), height: 4 (over x, core).
Axes of the slice: x: 2, y: 2, z: 4, core: 2. Of those that a mesh axis runs over, the one named last changes fastest.
Arguments:
- latents: bfloat16 [8, 24, 64, 1152], P('frame', 'height'), may hold values from -30 to 30
- qkv_weight: bfloat16 [2, 1152, 1728], replicated, as said below
- out_weight: bfloat16 [2, 576, 1152], replicated, may hold values from -0.25 to 0.25
Outputs:
- result: bfloat16 [8, 24, 64, 1152], P('frame', 'height')
Inputs may be any that keep to these rules, and one draw needn't show every extreme that they name: `qkv_weight`: entries lie within -0.2 to 0.2.
All inputs are finite; a program needn't handle non-finite values.
Results may differ from a plain program's by a relative error of at most 0.0095.
Values may be sent and summed in bfloat16 or wider, within the bound.
No kernel may reach another device: no remote copies, remote signals or barrier semaphores. Data moves between devices by JAX's collectives and lax.ppermute only.
A program may use at most 64 MiB of HBM per device.

v0:
```python
import jax
import jax.numpy as jnp
from jax import lax
from jax.sharding import PartitionSpec as P

HEAD_DIM = 72


def layer_norm(values):
    values = values.astype(jnp.float32)
    center = values - jnp.mean(values, axis=-1, keepdims=True)
    spread = jnp.mean(center * center, axis=-1, keepdims=True)
    return (center * lax.rsqrt(spread + 1e-06)).astype(jnp.bfloat16)


def project(tokens, weight):
    normed = layer_norm(tokens)
    flattened = normed.reshape(-1, normed.shape[-1])
    joined = jnp.dot(flattened, weight, preferred_element_type=jnp.float32)
    return joined.astype(jnp.bfloat16).reshape(tokens.shape[:-1] + (weight.shape[1],))


def attend(joined):
    length, batches = (joined.shape[0], joined.shape[1])
    inner_width = joined.shape[2] // 3
    head_count = inner_width // HEAD_DIM
    query_rows = joined[:, :, :inner_width].reshape(length, batches, head_count, HEAD_DIM)
    key_rows = joined[:, :, inner_width : 2 * inner_width].reshape(
        length, batches, head_count, HEAD_DIM
    )
    value_rows = joined[:, :, 2 * inner_width :].reshape(length, batches, head_count, HEAD_DIM)
    scores = jnp.einsum(
        "lbnd,mbnd->bnlm", query_rows, key_rows, preferred_element_type=jnp.float32
    ) * HEAD_DIM ** (-0.5)
    scores = scores - jnp.max(scores, axis=-1, keepdims=True)
    exponent = jnp.exp(scores)
    weights = (exponent / jnp.sum(exponent, axis=-1, keepdims=True)).astype(jnp.bfloat16)
    mixture = jnp.einsum("bnlm,mbnd->lbnd", weights, value_rows, preferred_element_type=jnp.float32)
    return mixture.reshape(length, batches, inner_width).astype(jnp.bfloat16)


def residual(tokens, mixture, weight):
    update = jnp.dot(
        mixture.reshape(-1, mixture.shape[-1]), weight, preferred_element_type=jnp.float32
    )
    return (tokens.astype(jnp.float32) + update.reshape(tokens.shape)).astype(jnp.bfloat16)


def frames_block(joined):
    length, single, places, triple = joined.shape
    mixture = attend(joined.reshape(length, single * places, triple))
    return mixture.reshape(length, single, places, triple // 3)


def per_device(latents, qkv_weight, out_weight):
    frames_dev, rows_dev, columns, feature_width = latents.shape
    frame_count = lax.axis_size("frame")
    rows_attend = jax.vmap(attend)
    rows_att = rows_attend(
        project(
            lax.all_to_all(latents, "height", split_axis=2, concat_axis=1, tiled=True),
            qkv_weight[0],
        )
    )
    rows_att = lax.all_to_all(rows_att, "height", split_axis=1, concat_axis=2, tiled=True)
    middle = residual(latents, rows_att, out_weight[0])
    places_dev = rows_dev * columns // frame_count
    grouped = middle.reshape(frames_dev, frame_count, places_dev, feature_width)
    frames_att = frames_block(
        project(
            lax.all_to_all(grouped, "frame", split_axis=1, concat_axis=0, tiled=True), qkv_weight[1]
        )
    )
    frames_att = lax.all_to_all(frames_att, "frame", split_axis=0, concat_axis=1, tiled=True)
    frames_att = frames_att.reshape(frames_dev, rows_dev, columns, frames_att.shape[-1])
    return residual(middle, frames_att, out_weight[1])


def solution(mesh):
    return jax.shard_map(
        per_device,
        mesh=mesh,
        in_specs=(P("frame", "height", None, None), P(), P()),
        out_specs=P("frame", "height", None, None),
        check_vma=False,
    )
```

profile of v0, /device:TPU:0, one launch (start us, length us, event | category | flops | bytes accessed | tf_op | source)
XLA Modules:
  0.0 113.4 jit_solution(6258203247795227640)
XLA Ops:
  0.0 1.7 %copy.33 = bf16[1,6,64,1152]{3,1,0,2:T(8,128)(2,1)S(1)} copy(bf16[1,6,64,1152]{3,2,1,0:T(8,128)(2,1)} %param.3) | data formatting | bytes 1769472 | tf_op args[0]
  1.7 0.0 copy-start.5
  1.7 20.1 %all_to_all.42 = bf16[1,6,64,1152]{3,1,0,2:T(8,128)(2,1)S(1)} all-to-all(bf16[1,6,64,1152]{3,1,0,2:T(8,128)(2,1)S(1)} %copy.33), channel_id=1, replica_groups=mesh['frame'=8,'height'=4] {'height'}, dimensions={2} | all-to-all | bytes 1769472 | tf_op jit(solution)/shard_map/all_to_all | solution.py:61
  21.8 0.1 copy.34
  21.9 0.2 fusion.24
  22.2 0.4 fusion.27
  22.5 0.3 fusion.28
  22.8 0.1 copy.35
  22.9 0.0 copy-done.5
  22.9 2.4 %fusion.12 = bf16[384,1728]{0,1:T(8,128)(2,1)S(1)} fusion(bf16[384,1152]{1,0:T(8,128)(2,1)S(1)} %bitcast.98, bf16[2,1152,1728]{1,2,0:T(8,128)(2,1)S(1)} %copy-done.5), kind=kOutput, calls=%fused_computation.14 | convolution fusion | flops 1529487360 | bytes 6193152 | tf_op jit(solution)/shard_map/dot_general | solution.py:19
  25.3 1.8 %copy.36 = bf16[384,1728]{1,0:T(8,128)(2,1)S(1)} copy(bf16[384,1728]{0,1:T(8,128)(2,1)S(1)} %fusion.12) | data formatting | bytes 2654208 | tf_op jit(solution)/shard_map/convert_element_type | solution.py:20
  27.1 0.3 fusion.68
  27.3 0.8 reshape.264
  28.1 0.8 reshape.265
  28.9 1.7 %reshape.263 = bf16[24,16,8,72]{3,2,1,0:T(8,128)(2,1)} reshape(bf16[1,24,16,576]{3,2,1,0:T(8,128)(2,1)S(1)} %get-tuple-element.8) | data formatting | bytes 884736 | tf_op jit(solution)/shard_map/reshape.7
  30.6 0.0 copy-start.3
  30.6 2.6 %fusion.69 = (f32[16,8,24]{2,1,0:T(8,128)S(1)}, f32[16,8,24,24]{2,3,1,0:T(8,128)}) fusion(bf16[24,16,8,72]{3,2,1,0:T(8,128)(2,1)S(1)} %reshape.265, bf16[24,16,8,72]{3,2,1,0:T(8,128)(2,1)S(1)} %reshape.264), kind=kOutput, calls=%fused_computation.65 | convolution fusion | flops 10838039 | bytes 1191936 | tf_op jit(solution)/shard_map/vmap()/sub | solution.py:35
  33.2 0.0 copy-done.3
  33.2 2.1 %fusion.37 = bf16[1,24,16,8,72]{4,1,3,2,0:T(8,128)(2,1)S(1)} fusion(f32[16,8,24,24]{2,3,1,0:T(8,128)} %get-tuple-element.12, bf16[24,16,8,72]{3,2,1,0:T(8,128)(2,1)S(1)} %copy-done.3, f32[16,8,24]{2,1,0:T(8,128)S(1)} %get-tuple-element.11), kind=kOutput, calls=%fused_computation.45 | convolution fusion | flops 10985472 | bytes 1191936 | tf_op jit(solution)/shard_map/vmap(bnlm,mbnd->lbnd)/dot_general | solution.py:38
  35.4 0.2 copy.41
  35.5 0.0 copy-start.2
  35.5 0.6 convert_element_type.136
  36.1 10.9 %all_to_all.43 = bf16[1,24,16,576]{3,2,0,1:T(8,128)(2,1)S(1)} all-to-all(bf16[1,24,16,576]{3,2,0,1:T(8,128)(2,1)S(1)} %bitcast.93), channel_id=1, replica_groups=mesh['frame'=8,'height'=4] {'height'}, dimensions={1} | all-to-all | bytes 884736 | tf_op jit(solution)/shard_map/all_to_all | solution.py:65
  47.0 0.0 copy-done.2
  47.0 2.3 %fusion.10 = bf16[1,6,64,1152]{3,2,1,0:T(8,128)(2,1)S(1)} fusion(bf16[6,64,576]{2,1,0:T(8,128)(2,1)S(1)} %bitcast.100, bf16[1,6,64,1152]{3,2,1,0:T(8,128)(2,1)S(1)} %copy-done.2, bf16[2,576,1152]{2,1,0:T(8,128)(2,1)} %param.5), kind=kOutput, calls=%fused_computation.12 | convolution fusion | flops 510935040 | bytes 3538944 | tf_op jit(solution)/shard_map/dot_general | solution.py:43
  49.3 0.0 copy-start
  49.3 28.1 %all_to_all.44 = bf16[1,8,48,1152]{3,2,0,1:T(8,128)(2,1)S(1)} all-to-all(bf16[1,8,48,1152]{3,2,0,1:T(8,128)(2,1)S(1)} %bitcast.96), channel_id=1, replica_groups=mesh['frame'=8,'height'=4] {'frame'}, dimensions={1} | all-to-all | bytes 1769472 | tf_op jit(solution)/shard_map/all_to_all | solution.py:71
  77.5 0.2 convert_reduce_fusion
  77.7 0.4 fusion.22
  78.0 0.0 copy-done
  78.1 0.3 fusion.19
  78.4 4.5 %fusion.15 = bf16[384,1728]{0,1:T(8,128)(2,1)S(1)} fusion(bf16[384,1152]{1,0:T(8,128)(2,1)S(1)} %bitcast.97, bf16[2,1152,1728]{1,2,0:T(8,128)(2,1)} %param.4), kind=kOutput, calls=%fused_computation.15 | convolution fusion | flops 1529487360 | bytes 6193152 | tf_op jit(solution)/shard_map/dot_general | solution.py:19
  82.8 1.8 %copy.45 = bf16[384,1728]{1,0:T(8,128)(2,1)S(1)} copy(bf16[384,1728]{0,1:T(8,128)(2,1)S(1)} %fusion.15) | data formatting | bytes 2654208 | tf_op jit(solution)/shard_map/convert_element_type | solution.py:20
  84.6 0.3 fusion.67
  84.9 0.8 reshape.269
  85.7 0.8 reshape.270
  86.5 1.7 %reshape.268 = bf16[8,48,8,72]{3,2,1,0:T(8,128)(2,1)} reshape(bf16[8,48,576]{2,1,0:T(8,128)(2,1)S(1)} %get-tuple-element.5) | data formatting | bytes 884736 | tf_op jit(solution)/shard_map/reshape | solution.py:31
  88.1 0.0 copy-start.4
  88.1 2.8 %fusion.74 = (f32[48,8,8]{2,1,0:T(8,128)S(1)}, f32[48,8,8,8]{2,3,1,0:T(8,128)}) fusion(bf16[8,48,8,72]{3,2,1,0:T(8,128)(2,1)S(1)} %reshape.270, bf16[8,48,8,72]{3,2,1,0:T(8,128)(2,1)S(1)} %reshape.269), kind=kOutput, calls=%fused_computation.66 | convolution fusion | flops 3612679 | bytes 995328 | tf_op jit(solution)/shard_map/sub | solution.py:35
  90.9 0.0 copy-done.4
  90.9 2.2 %fusion.38 = bf16[8,48,8,72]{3,0,2,1:T(8,128)(2,1)S(1)} fusion(f32[48,8,8,8]{2,3,1,0:T(8,128)} %get-tuple-element.14, bf16[8,48,8,72]{3,2,1,0:T(8,128)(2,1)S(1)} %copy-done.4, f32[48,8,8]{2,1,0:T(8,128)S(1)} %get-tuple-element.13), kind=kOutput, calls=%fused_computation.46 | convolution fusion | flops 3809280 | bytes 995328 | tf_op jit(solution)/shard_map/bnlm,mbnd->lbnd/dot_general | solution.py:38
  93.1 0.0 copy-start.1
  93.1 0.1 copy.50
  93.2 0.6 convert_element_type.147
  93.8 16.4 %all_to_all.45 = bf16[8,1,48,576]{3,2,1,0:T(8,128)(2,1)S(1)} all-to-all(bf16[8,1,48,576]{3,2,1,0:T(8,128)(2,1)S(1)} %bitcast.95), channel_id=1, replica_groups=mesh['frame'=8,'height'=4] {'frame'}, dimensions={0} | all-to-all | bytes 884736 | tf_op jit(solution)/shard_map/all_to_all | solution.py:74
  110.2 0.0 copy-done.1
  110.2 3.2 %fusion.11 = bf16[1,6,64,1152]{3,2,1,0:T(8,128)(2,1)} fusion(bf16[6,64,576]{2,1,0:T(8,128)(2,1)S(1)} %bitcast.99, bf16[1,6,64,1152]{3,2,1,0:T(8,128)(2,1)S(1)} %copy-done.1, bf16[2,576,1152]{2,1,0:T(8,128)(2,1)} %param.5), kind=kOutput, calls=%fused_computation.13 | convolution fusion | flops 510935040 | bytes 3538944 | tf_op jit(solution)/shard_map/dot_general | solution.py:43
  (5 shorter events, 0.1 us)
Async XLA Ops:
  1.7 21.2 %copy-start.5 = (bf16[2,1152,1728]{1,2,0:T(8,128)(2,1)S(1)}, bf16[2,1152,1728]{1,2,0:T(8,128)(2,1)}, u32[]{:S(2)}) copy-start(bf16[2,1152,1728]{1,2,0:T(8,128)(2,1)} %param.4) | copy-start | bytes 23887876
  30.6 2.6 %copy-start.3 = (bf16[24,16,8,72]{3,2,1,0:T(8,128)(2,1)S(1)}, bf16[24,16,8,72]{3,2,1,0:T(8,128)(2,1)}, u32[]{:S(2)}) copy-start(bf16[24,16,8,72]{3,2,1,0:T(8,128)(2,1)} %reshape.263) | copy-start | bytes 1327108
  35.5 11.5 %copy-start.2 = (bf16[1,6,64,1152]{3,2,1,0:T(8,128)(2,1)S(1)}, bf16[1,6,64,1152]{3,2,1,0:T(8,128)(2,1)}, u32[]{:S(2)}) copy-start(bf16[1,6,64,1152]{3,2,1,0:T(8,128)(2,1)} %param.3) | copy-start | bytes 2654212
  49.3 28.7 %copy-start = (bf16[1,6,64,1152]{3,2,1,0:T(8,128)(2,1)}, bf16[1,6,64,1152]{3,2,1,0:T(8,128)(2,1)S(1)}, u32[]{:S(2)}) copy-start(bf16[1,6,64,1152]{3,2,1,0:T(8,128)(2,1)S(1)} %fusion.10) | copy-start | bytes 2654212
  88.1 2.8 %copy-start.4 = (bf16[8,48,8,72]{3,2,1,0:T(8,128)(2,1)S(1)}, bf16[8,48,8,72]{3,2,1,0:T(8,128)(2,1)}, u32[]{:S(2)}) copy-start(bf16[8,48,8,72]{3,2,1,0:T(8,128)(2,1)} %reshape.268) | copy-start | bytes 1327108
  93.1 17.1 %copy-start.1 = (bf16[1,6,64,1152]{3,2,1,0:T(8,128)(2,1)S(1)}, bf16[1,6,64,1152]{3,2,1,0:T(8,128)(2,1)}, u32[]{:S(2)}) copy-start(bf16[1,6,64,1152]{3,2,1,0:T(8,128)(2,1)} %copy-done) | copy-start | bytes 2654212
where the time goes:
time: 114 us; the launch traced here: 113 us
  blocking collectives  75.5 us (66%)
  matrix products  22 us (19%)
  local copies, waits for them, and re-layouts  13.9 us (12%)
  other arithmetic  1.71 us (2%)
    all_to_all x1, blocking collectives, per_device(): lax.all_to_all(grouped, 'frame', split_axis=1, concat_axis=0, tiled=True)  28.1 us
    all_to_all x1, blocking collectives, per_device(): lax.all_to_all(latents, 'height', split_axis=2, concat_axis=1, tiled=True)  20.1 us
    all_to_all x1, blocking collectives, per_device(): lax.all_to_all(frames_att, 'frame', split_axis=0, concat_axis=1, tiled=True)  16.4 us
    all_to_all x1, blocking collectives, per_device(): lax.all_to_all(rows_att, 'height', split_axis=1, concat_axis=2, tiled=True)  10.9 us
    dot_general x2, matrix products, project(): joined = jnp.dot(flattened, weight, preferred_element_type=jnp.float32)  6.84 us
    dot_general x2, matrix products, residual(): jnp.dot(mixture.reshape(-1, mixture.shape[-1]), weight, preferred_element...  5.45 us
    sub x2, matrix products, attend(): scores = scores - jnp.max(scores, axis=-1, keepdims=True)  5.41 us
    dot_general x2, matrix products, attend(): jnp.einsum('bnlm,mbnd->lbnd', weights, value_rows, preferred_element_type...  4.31 us

commit v1 on v0

--- a/solution.py
+++ b/solution.py
@@ -71,7 +71,12 @@
             lax.all_to_all(grouped, "frame", split_axis=1, concat_axis=0, tiled=True), qkv_weight[1]
         )
     )
-    frames_att = lax.all_to_all(frames_att, "frame", split_axis=0, concat_axis=1, tiled=True)
+    frames_att = jnp.concatenate(
+        lax.all_to_all(
+            jnp.stack(jnp.split(frames_att, lax.axis_size("frame"), axis=0)), "frame", 0, 0
+        ),
+        axis=1,
+    )
     frames_att = frames_att.reshape(frames_dev, rows_dev, columns, frames_att.shape[-1])
     return residual(middle, frames_att, out_weight[1])
 

time: 114 us -> 119 us (1.044)
  local copies, waits for them, and re-layouts: 13.9 us -> 18.9 us
    split x0 -> x1, local copies, waits for them, and re-layouts: none -> 4.56 us  [per_device(): jnp.split(frames_att, lax.axis_size('frame'), axis=0)]
    another operation x3 -> x12, local copies, waits for them, and re-layouts: 3.23 us -> 4.27 us
where the time goes in v1:
time: 119 us; the launch traced here: 118 us
  blocking collectives  75.5 us (63%)
  matrix products  22 us (18%)
  local copies, waits for them, and re-layouts  18.9 us (16%)
  other arithmetic  1.71 us (1%)
    all_to_all x1, blocking collectives, per_device(): lax.all_to_all(grouped, 'frame', split_axis=1, concat_axis=0, tiled=True)  28.1 us
    all_to_all x1, blocking collectives, per_device(): lax.all_to_all(latents, 'height', split_axis=2, concat_axis=1, tiled=True)  20.1 us
    all_to_all x1, blocking collectives, per_device(): lax.all_to_all(jnp.stack(jnp.split(frames_att, lax.axis_size('frame'), ax...  16.4 us
    all_to_all x1, blocking collectives, per_device(): lax.all_to_all(rows_att, 'height', split_axis=1, concat_axis=2, tiled=True)  10.9 us
    dot_general x2, matrix products, project(): joined = jnp.dot(flattened, weight, preferred_element_type=jnp.float32)  6.84 us
    dot_general x2, matrix products, residual(): jnp.dot(mixture.reshape(-1, mixture.shape[-1]), weight, preferred_element...  5.45 us
    sub x2, matrix products, attend(): scores = scores - jnp.max(scores, axis=-1, keepdims=True)  5.41 us
    split x1, local copies, waits for them, and re-layouts, per_device(): jnp.split(frames_att, lax.axis_size('frame'), axis=0)  4.56 us

profile of v1, /device:TPU:0, one launch (start us, length us, event | category | flops | bytes accessed | tf_op | source)
XLA Modules:
  0.0 118.4 jit_solution(10630902428151552163)
XLA Ops:
  0.0 1.7 %copy.31 = bf16[1,6,64,1152]{3,1,0,2:T(8,128)(2,1)S(1)} copy(bf16[1,6,64,1152]{3,2,1,0:T(8,128)(2,1)} %param.3) | data formatting | bytes 1769472 | tf_op args[0]
  1.7 0.0 copy-start.5
  1.7 20.1 %all_to_all.38 = bf16[1,6,64,1152]{3,1,0,2:T(8,128)(2,1)S(1)} all-to-all(bf16[1,6,64,1152]{3,1,0,2:T(8,128)(2,1)S(1)} %copy.31), channel_id=1, replica_groups=mesh['frame'=8,'height'=4] {'height'}, dimensions={2} | all-to-all | bytes 1769472 | tf_op jit(solution)/shard_map/all_to_all | solution.py:61
  21.8 0.1 copy.32
  21.9 0.2 fusion.24
  22.2 0.4 fusion.27
  22.5 0.3 fusion.28
  22.8 0.1 copy.33
  22.9 0.0 copy-done.5
  22.9 2.4 %fusion.12 = bf16[384,1728]{0,1:T(8,128)(2,1)S(1)} fusion(bf16[384,1152]{1,0:T(8,128)(2,1)S(1)} %bitcast.94, bf16[2,1152,1728]{1,2,0:T(8,128)(2,1)S(1)} %copy-done.5), kind=kOutput, calls=%fused_computation.14 | convolution fusion | flops 1529487360 | bytes 6193152 | tf_op jit(solution)/shard_map/dot_general | solution.py:19
  25.3 1.8 %copy.34 = bf16[384,1728]{1,0:T(8,128)(2,1)S(1)} copy(bf16[384,1728]{0,1:T(8,128)(2,1)S(1)} %fusion.12) | data formatting | bytes 2654208 | tf_op jit(solution)/shard_map/convert_element_type | solution.py:20
  27.1 0.3 fusion.68
  27.3 0.8 reshape.282
  28.1 0.8 reshape.283
  28.9 1.7 %reshape.281 = bf16[24,16,8,72]{3,2,1,0:T(8,128)(2,1)} reshape(bf16[1,24,16,576]{3,2,1,0:T(8,128)(2,1)S(1)} %get-tuple-element.16) | data formatting | bytes 884736 | tf_op jit(solution)/shard_map/reshape.7
  30.6 2.6 %fusion.69 = (f32[16,8,24]{2,1,0:T(8,128)S(1)}, f32[16,8,24,24]{2,3,1,0:T(8,128)}) fusion(bf16[24,16,8,72]{3,2,1,0:T(8,128)(2,1)S(1)} %reshape.283, bf16[24,16,8,72]{3,2,1,0:T(8,128)(2,1)S(1)} %reshape.282), kind=kOutput, calls=%fused_computation.81 | convolution fusion | flops 10838039 | bytes 1191936 | tf_op jit(solution)/shard_map/vmap()/sub | solution.py:35
  33.2 0.0 copy-done.3
  33.2 2.1 %fusion.37 = bf16[1,24,16,8,72]{4,1,3,2,0:T(8,128)(2,1)S(1)} fusion(f32[16,8,24,24]{2,3,1,0:T(8,128)} %get-tuple-element.20, bf16[24,16,8,72]{3,2,1,0:T(8,128)(2,1)S(1)} %copy-done.3, f32[16,8,24]{2,1,0:T(8,128)S(1)} %get-tuple-element.19), kind=kOutput, calls=%fused_computation.45 | convolution fusion | flops 10985472 | bytes 1191936 | tf_op jit(solution)/shard_map/vmap(bnlm,mbnd->lbnd)/dot_general | solution.py:38
  35.4 0.2 copy.39
  35.5 0.0 copy-start.2
  35.5 0.6 convert_element_type.127
  36.1 10.9 %all_to_all.39 = bf16[1,24,16,576]{3,2,0,1:T(8,128)(2,1)S(1)} all-to-all(bf16[1,24,16,576]{3,2,0,1:T(8,128)(2,1)S(1)} %bitcast.90), channel_id=1, replica_groups=mesh['frame'=8,'height'=4] {'height'}, dimensions={1} | all-to-all | bytes 884736 | tf_op jit(solution)/shard_map/all_to_all | solution.py:65
  47.0 2.3 %fusion.10 = bf16[1,6,64,1152]{3,2,1,0:T(8,128)(2,1)S(1)} fusion(bf16[6,64,576]{2,1,0:T(8,128)(2,1)S(1)} %bitcast.96, bf16[1,6,64,1152]{3,2,1,0:T(8,128)(2,1)S(1)} %copy-done.2, bf16[2,576,1152]{2,1,0:T(8,128)(2,1)} %param.5), kind=kOutput, calls=%fused_computation.12 | convolution fusion | flops 510935040 | bytes 3538944 | tf_op jit(solution)/shard_map/dot_general | solution.py:43
  49.3 0.0 copy-start
  49.3 28.1 %all_to_all.40 = bf16[1,8,48,1152]{3,2,0,1:T(8,128)(2,1)S(1)} all-to-all(bf16[1,8,48,1152]{3,2,0,1:T(8,128)(2,1)S(1)} %bitcast.92), channel_id=1, replica_groups=mesh['frame'=8,'height'=4] {'frame'}, dimensions={1} | all-to-all | bytes 1769472 | tf_op jit(solution)/shard_map/all_to_all | solution.py:71
  77.5 0.2 convert_reduce_fusion
  77.7 0.4 fusion.22
  78.1 0.3 fusion.19
  78.4 4.5 %fusion.15 = bf16[384,1728]{0,1:T(8,128)(2,1)S(1)} fusion(bf16[384,1152]{1,0:T(8,128)(2,1)S(1)} %bitcast.93, bf16[2,1152,1728]{1,2,0:T(8,128)(2,1)} %param.4), kind=kOutput, calls=%fused_computation.15 | convolution fusion | flops 1529487360 | bytes 6193152 | tf_op jit(solution)/shard_map/dot_general | solution.py:19
  82.8 1.8 %copy.43 = bf16[384,1728]{1,0:T(8,128)(2,1)S(1)} copy(bf16[384,1728]{0,1:T(8,128)(2,1)S(1)} %fusion.15) | data formatting | bytes 2654208 | tf_op jit(solution)/shard_map/convert_element_type | solution.py:20
  84.6 0.3 fusion.67
  84.9 0.8 reshape.287
  85.7 0.8 reshape.288
  86.5 1.7 %reshape.286 = bf16[8,48,8,72]{3,2,1,0:T(8,128)(2,1)} reshape(bf16[8,48,576]{2,1,0:T(8,128)(2,1)S(1)} %get-tuple-element.13) | data formatting | bytes 884736 | tf_op jit(solution)/shard_map/reshape | solution.py:31
  88.1 2.8 %fusion.74 = (f32[48,8,8]{2,1,0:T(8,128)S(1)}, f32[48,8,8,8]{2,3,1,0:T(8,128)}) fusion(bf16[8,48,8,72]{3,2,1,0:T(8,128)(2,1)S(1)} %reshape.288, bf16[8,48,8,72]{3,2,1,0:T(8,128)(2,1)S(1)} %reshape.287), kind=kOutput, calls=%fused_computation.82 | convolution fusion | flops 3612679 | bytes 995328 | tf_op jit(solution)/shard_map/sub | solution.py:35
  90.9 2.2 %fusion.38 = bf16[8,48,8,72]{3,0,2,1:T(8,128)(2,1)S(1)} fusion(f32[48,8,8,8]{2,3,1,0:T(8,128)} %get-tuple-element.22, bf16[8,48,8,72]{3,2,1,0:T(8,128)(2,1)S(1)} %copy-done.4, f32[48,8,8]{2,1,0:T(8,128)S(1)} %get-tuple-element.21), kind=kOutput, calls=%fused_computation.46 | convolution fusion | flops 3809280 | bytes 995328 | tf_op jit(solution)/shard_map/bnlm,mbnd->lbnd/dot_general | solution.py:38
  93.1 4.6 %slice_reduce_fusion = (bf16[48,8,72]{2,1,0:T(8,128)(2,1)S(1)}, bf16[48,8,72]{2,1,0:T(8,128)(2,1)S(1)}, bf16[48,8,72]{2,1,0:T(8,128)(2,1)S(1)}, bf16[48,8,72]{2,...) fusion(bf16[8,48,8,72]{3,0,2,1:T(8,128)(2,1)S(1)} %fusion.38), kind=kLoop, calls=%fused_computation.55 | loop fusion | bytes 884736 | tf_op jit(solution)/shard_map/split | solution.py:76
  97.7 0.0 copy-start.1
  97.7 0.1 stack.27
  97.8 0.1 stack.28
  98.0 0.1 stack.29
  98.1 0.1 stack.30
  98.2 0.1 stack.31
  98.4 0.1 stack.32
  98.5 0.1 stack.33
  98.6 0.1 stack.34
  98.9 16.4 %all_to_all.41 = bf16[8,1,1,48,576]{4,3,2,1,0:T(8,128)(2,1)S(1)} all-to-all(bf16[8,1,1,48,576]{4,3,2,1,0:T(8,128)(2,1)S(1)} %constant_dynamic-update-slice_fusion), channel_id=1, replica_groups=mesh['frame'=8,'height'=4] {'frame'}, dimensions={0} | all-to-all | bytes 884736 | tf_op jit(solution)/shard_map/all_to_all | solution.py:75
  115.3 3.2 %fusion.11 = bf16[1,6,64,1152]{3,2,1,0:T(8,128)(2,1)} fusion(bf16[6,64,576]{2,1,0:T(8,128)(2,1)S(1)} %bitcast.95, bf16[1,6,64,1152]{3,2,1,0:T(8,128)(2,1)S(1)} %copy-done.1, bf16[2,576,1152]{2,1,0:T(8,128)(2,1)} %param.5), kind=kOutput, calls=%fused_computation.13 | convolution fusion | flops 510935040 | bytes 3538944 | tf_op jit(solution)/shard_map/dot_general | solution.py:43
  (19 shorter events, 0.2 us)
Async XLA Ops:
  1.7 21.2 %copy-start.5 = (bf16[2,1152,1728]{1,2,0:T(8,128)(2,1)S(1)}, bf16[2,1152,1728]{1,2,0:T(8,128)(2,1)}, u32[]{:S(2)}) copy-start(bf16[2,1152,1728]{1,2,0:T(8,128)(2,1)} %param.4) | copy-start | bytes 23887876
  30.6 2.6 %copy-start.3 = (bf16[24,16,8,72]{3,2,1,0:T(8,128)(2,1)S(1)}, bf16[24,16,8,72]{3,2,1,0:T(8,128)(2,1)}, u32[]{:S(2)}) copy-start(bf16[24,16,8,72]{3,2,1,0:T(8,128)(2,1)} %reshape.281) | copy-start | bytes 1327108
  35.5 11.5 %copy-start.2 = (bf16[1,6,64,1152]{3,2,1,0:T(8,128)(2,1)S(1)}, bf16[1,6,64,1152]{3,2,1,0:T(8,128)(2,1)}, u32[]{:S(2)}) copy-start(bf16[1,6,64,1152]{3,2,1,0:T(8,128)(2,1)} %param.3) | copy-start | bytes 2654212
  49.3 28.7 %copy-start = (bf16[1,6,64,1152]{3,2,1,0:T(8,128)(2,1)}, bf16[1,6,64,1152]{3,2,1,0:T(8,128)(2,1)S(1)}, u32[]{:S(2)}) copy-start(bf16[1,6,64,1152]{3,2,1,0:T(8,128)(2,1)S(1)} %fusion.10) | copy-start | bytes 2654212
  88.1 2.8 %copy-start.4 = (bf16[8,48,8,72]{3,2,1,0:T(8,128)(2,1)S(1)}, bf16[8,48,8,72]{3,2,1,0:T(8,128)(2,1)}, u32[]{:S(2)}) copy-start(bf16[8,48,8,72]{3,2,1,0:T(8,128)(2,1)} %reshape.286) | copy-start | bytes 1327108
  97.7 17.6 %copy-start.1 = (bf16[1,6,64,1152]{3,2,1,0:T(8,128)(2,1)S(1)}, bf16[1,6,64,1152]{3,2,1,0:T(8,128)(2,1)}, u32[]{:S(2)}) copy-start(bf16[1,6,64,1152]{3,2,1,0:T(8,128)(2,1)} %copy-done) | copy-start | bytes 2654212
